TPU v7x, 32 devices: a whole 2x2x4 slice. The times are simulated.
32 devices in a mesh: ctx: 8 (over y, x, core), kvh: 4 (over z).
Axes of the slice: x: 2, y: 2, z: 4, core: 2. Of those that a mesh axis runs over, the one named last changes fastest.
Arguments:
- queries: float32 [8, 256, 64, 128], P('ctx', None, 'kvh'), may hold values from -64 to 64
- cache_keys: float32 [8, 4096, 128], P('kvh', 'ctx'), may hold values from -16 to 16
- cache_values: float32 [8, 4096, 128], P('kvh', 'ctx'), may hold values from -6 to 6
- bounds: int32 [8, 3], replicated, may hold values from 0 to 2048, as said below
Outputs:
- attended: float32 [8, 256, 64, 128], P('ctx', None, 'kvh')
Inputs may be any that keep to these rules, and one draw needn't show every extreme that they name: bounds[b] = (s, w, l) with 2 <= s <= 64, 0 <= w < 256, 1792 < l <= 2048; block 0 has s = 64, w = 0, l = 2048.
All inputs are finite; a program needn't handle non-finite values.
Results may differ from a plain program's by a relative error of at most 0.0003.
Values sent between devices are 32-bit elements; how exact they have to be, the bound alone decides.
No kernel may reach another device: no remote copies, remote signals or barrier semaphores. Data moves between devices by JAX's collectives and lax.ppermute only.
A program may use at most 64 MiB of HBM per device.

v0:
```python
import functools
import math

import jax
import jax.numpy as jnp
from jax import lax
from jax.experimental import pallas as pl
from jax.experimental.pallas import tpu as pltpu
from jax.sharding import PartitionSpec as P

SINK = 64
SPAN = 4
LANES = 128
BLOCK_ROWS = 1024
VMEM_LIMIT = 20 << 20
PACK_LIMIT = 58 << 20
NEG = -1e30


BF16 = jnp.bfloat16
F32 = jnp.float32
VMEM = pl.BlockSpec(memory_space=pltpu.VMEM)
SMEM = pl.BlockSpec(memory_space=pltpu.SMEM)
HBM = pl.BlockSpec(memory_space=pltpu.HBM)
ANY = pl.BlockSpec(memory_space=pl.ANY)


def split(x):
    high = x.astype(BF16)
    return high, (x - high.astype(F32)).astype(BF16)


def exchange(x, source, count):
    return lax.ppermute(x, "ctx", [(source(i) % count, i) for i in range(count)])


def first_source(i):
    return i + (4, 2, -1, 3)[i % 4]


def second_source(i):
    return i + (3, 4, 4, -3)[i % 4]


def pair_source(i):
    return i ^ 1


PIECES = (
    (("own_pair", 1), ("first", 2), ("own_pair", 1), ("first", 3)),
    (("first_pair", 3), ("first_pair", 3), ("second", 3), ("second", 1)),
    (("second", 2), ("second_pair", 1), ("second_pair", 2), ("second_pair", 2)),
)


def pick(role, values):
    result = values[0]
    for r in range(1, len(values)):
        result = jnp.where(role == r, values[r], result)
    return result


def make_step(*, jobs, pieces, sink, fresh, final, rows_t, group, head_size, slots, total):
    names = list(dict.fromkeys(n for piece in pieces for n, _ in piece))
    rows = rows_t * group
    block = min(BLOCK_ROWS, rows)
    block_t = block // group
    chunks = rows // block
    width = slots * len(pieces)
    scale = math.log2(math.e) / math.sqrt(head_size)
    count = len(jobs)

    def kernel(*refs):
        refs = list(refs)

        def take(n):
            front, refs[:] = refs[:n], refs[n:]
            return front

        place_ref, bounds_ref, q_ref = take(3)
        sources = {n: take(2 if fresh else count) for n in names}

        def source(job, name, j):
            return sources[name][job][j]

        sink_refs = [take(count) for _ in range(sink)]
        states_in = [take(2) for _ in jobs] if not fresh else None
        if final == 2:
            take(1)
        if final:
            (out_ref,) = take(1)
        else:
            states_out = [take(2) for _ in jobs]
        (sink_out,) = take(1) if fresh else (None,)
        k_cat, v_cat = take(2)
        ks_cat, vs_cat = take(2) if sink else (None, None)
        o_buf, o_sem = take(2) if final else (None, None)
        loads = {}
        if fresh:
            kv_buf, sems = take(2)
            for job, head in enumerate(jobs):
                loads[job] = [
                    pltpu.make_async_copy(ref.at[head], kv_buf.at[job, j], sems.at[job, j])
                    for j, ref in enumerate(sources["self"])
                ]
                for copy in loads[job]:
                    copy.start()
            sources = {"self": [kv_buf.at[job] for job in range(count)]}

        place = place_ref[0]
        role = lax.rem(place, 4)
        first, lower, upper = (bounds_ref[j, place] for j in range(3))
        lanes_half = lax.broadcasted_iota(jnp.int32, (1, LANES), 1) < SINK

        def load(job, piece, j):
            own_names = list(dict.fromkeys(n for n, _ in piece))
            value = source(job, own_names[0], j)
            for name in own_names[1:]:
                chosen = functools.reduce(jnp.logical_or, [role == r for r in range(4) if piece[r][0] == name])
                value = jnp.where(chosen, source(job, name, j), value)
            return value

        def prepare(job):
            for number, piece in enumerate(pieces):
                part = slice(number * slots, (number + 1) * slots)
                distance = pick(role, [d for _, d in piece])
                offset = distance * slots + lax.broadcasted_iota(jnp.int32, (slots, LANES), 0)
                lane = lax.broadcasted_iota(jnp.int32, (slots, LANES), 1)
                hidden = (lane == 0) & ((offset < lower) | (offset >= upper))
                high, low = split(load(job, piece, 0))
                mask = jnp.where(hidden, NEG, 0.0).astype(BF16)
                for j, value in enumerate((high, high, low, mask)):
                    k_cat[job, part, j * LANES : (j + 1) * LANES] = value
                for j, value in enumerate(split(load(job, piece, 1))):
                    v_cat[job, part, j * LANES : (j + 1) * LANES] = value
            if sink:

                def load_sink(j):
                    value = sink_refs[0][job][j, :SINK]
                    for r in range(1, sink):
                        value = jnp.where(place == r + 1, sink_refs[r][job][j, :SINK], value)
                    return value

                slot = lax.rem(lax.broadcasted_iota(jnp.int32, (2 * SINK, LANES), 0), SINK)
                lane = lax.broadcasted_iota(jnp.int32, (2 * SINK, LANES), 1)
                behind = slot - place * slots
                behind = jnp.where(behind < 0, behind + total, behind)
                seen = (slot < first) & ((behind < lower) | (behind >= upper))
                mask = jnp.where((lane == 0) & jnp.logical_not(seen), NEG, 0.0).astype(BF16)
                high, low = (jnp.concatenate([x, x]) for x in split(load_sink(0)))
                for j, value in enumerate((high, high, low, mask)):
                    ks_cat[job, :, j * LANES : (j + 1) * LANES] = value
                zero = jnp.zeros((SINK, LANES), BF16)
                high, low = split(load_sink(1))
                for j, value in enumerate(((high, high), (low, zero))):
                    vs_cat[job, :, j * LANES : (j + 1) * LANES] = jnp.concatenate(value)

        def scores_of(query, keys):
            return lax.dot_general(query, keys, (((1,), (1,)), ((), ())), preferred_element_type=F32)

        def mix(weights, values):
            return lax.dot_general(weights, values, (((1,), (0,)), ((), ())), preferred_element_type=F32)

        def by_halves(product, left, right):
            half = left.shape[0] // 2
            return jnp.concatenate([product(left[:half], right), product(left[half:], right)])

        def groups(x):
            return [x[:, j * LANES : (j + 1) * LANES] for j in range(width // LANES)]

        copies = []
        for job, head in enumerate(jobs):
            for copy in loads.get(job, ()):
                copy.wait()
            if fresh:
                for j in range(2):
                    sink_out[job, j] = source(job, "self", j)[:SINK]
            prepare(job)
            for chunk in range(chunks):
                here = pl.ds(chunk * block, block)
                query = q_ref[pl.ds(chunk * block_t, block_t), head * group : (head + 1) * group]
                high, low = split(query.reshape(block, head_size) * scale)
                ones = jnp.ones((block, LANES), BF16)
                query = jnp.concatenate([high, low, high, ones], axis=1)
                scores = scores_of(query, k_cat[job])
                top = functools.reduce(jnp.maximum, groups(scores))
                if sink:
                    sink_scores = by_halves(scores_of, query, ks_cat[job])
                    top = jnp.maximum(top, sink_scores)
                top = jnp.max(top, axis=1, keepdims=True)
                if fresh:
                    top = jnp.broadcast_to(top, (block, LANES))
                else:
                    old_top = states_in[job][1][here, :LANES]
                    top = jnp.maximum(top, old_top)
                    shrink = jnp.exp2(old_top - top)
                weights = jnp.exp2(scores - jnp.tile(top, (1, width // LANES)))
                sums = functools.reduce(jnp.add, groups(weights))
                high, low = split(weights)
                mixed = mix(high, v_cat[job])
                if sink:
                    weights = jnp.exp2(sink_scores - top)
                    sums = sums + jnp.where(lanes_half, weights, 0.0)
                    rest = weights - weights.astype(BF16).astype(F32)
                    mixed = mixed + by_halves(mix, jnp.where(lanes_half, weights, rest).astype(BF16), vs_cat[job])
                mixed = mixed[:, :LANES] + mixed[:, LANES:] + mix(low, v_cat[job, :, :LANES])
                if not fresh:
                    sums = sums + states_in[job][1][here, LANES:] * shrink
                    mixed = mixed + states_in[job][0][here] * shrink
                if final:
                    sums = jnp.sum(sums, axis=1, keepdims=True)
                    o_buf[chunk] = (mixed / sums).reshape(block_t, group, head_size)
                    copy = pltpu.make_async_copy(
                        o_buf.at[chunk],
                        out_ref.at[pl.ds(chunk * block_t, block_t), pl.ds(head * group, group)],
                        o_sem.at[chunk],
                    )
                    copy.start()
                    copies.append(copy)
                else:
                    acc_out, stat_out = states_out[job]
                    acc_out[here] = mixed
                    stat_out[here, :LANES] = top
                    stat_out[here, LANES:] = sums
        for copy in copies:
            copy.wait()

    taken = 2 if fresh else len(names) * count + count * sink + 2 * count
    in_specs = [SMEM, SMEM, VMEM] + [ANY if fresh else VMEM] * taken
    in_specs += [ANY] * (final == 2)
    scratch = [pltpu.VMEM((count, width, 4 * LANES), BF16), pltpu.VMEM((count, width, 2 * LANES), BF16)]
    if sink:
        scratch += [pltpu.VMEM((count, 2 * SINK, n * LANES), BF16) for n in (4, 2)]
    if final:
        scratch += [pltpu.VMEM((chunks, block_t, group, head_size), F32), pltpu.SemaphoreType.DMA((chunks,))]

    if fresh:
        scratch += [pltpu.VMEM((count, 2, slots, head_size), F32), pltpu.SemaphoreType.DMA((count, 2))]

    def call(queries, *args):
        if final:
            out_shape, out_specs = jax.ShapeDtypeStruct(queries.shape, F32), ANY
        else:
            out_shape = [
                jax.ShapeDtypeStruct((rows, head_size), F32),
                jax.ShapeDtypeStruct((rows, 2 * LANES), F32),
            ] * count
            out_specs = [VMEM, VMEM] * count
            if fresh:
                out_shape.append(jax.ShapeDtypeStruct((count, 2, SINK, head_size), F32))
                out_specs.append(VMEM)
        return pl.pallas_call(
            kernel,
            out_shape=out_shape,
            in_specs=in_specs,
            out_specs=out_specs,
            scratch_shapes=scratch,
            input_output_aliases={len(in_specs) - 1: 0} if final == 2 else {},
            compiler_params=pltpu.CompilerParams(vmem_limit_bytes=VMEM_LIMIT),
            cost_estimate=pl.CostEstimate(
                flops=count * rows * width * 2048, bytes_accessed=4 << 20, transcendentals=count * rows * width
            ),
        )(*args[:2], queries, *args[2:])

    return names, call


def pass_on(place, pair, came):
    def kernel(place_ref, pair_ref, came_ref, out_ref):
        out_ref[...] = jnp.where(lax.rem(place_ref[0], 4) == 3, pair_ref[...], came_ref[...])

    return pl.pallas_call(
        kernel,
        out_shape=jax.ShapeDtypeStruct(came.shape, F32),
        in_specs=[SMEM, VMEM, VMEM],
        out_specs=VMEM,
        compiler_params=pltpu.CompilerParams(vmem_limit_bytes=4 << 20),
        cost_estimate=pl.CostEstimate(flops=0, bytes_accessed=2 << 20, transcendentals=0),
    )(place, pair, came)


def pack(keys, values):
    heads, slots, head_size = keys.shape

    def kernel(k_ref, v_ref, *refs):
        outs, (buf, sems) = refs[:heads], refs[heads:]
        parts = [(h, j, ref) for h in range(heads) for j, ref in enumerate((k_ref, v_ref))]
        loads = [pltpu.make_async_copy(ref.at[h], buf.at[h, j], sems.at[h, j, 0]) for h, j, ref in parts]
        stores = [pltpu.make_async_copy(buf.at[h, j], outs[h].at[j], sems.at[h, j, 1]) for h, j, _ in parts]
        for load in loads:
            load.start()
        for load, store in zip(loads, stores):
            load.wait()
            store.start()
        for store in stores:
            store.wait()

    return pl.pallas_call(
        kernel,
        out_shape=[jax.ShapeDtypeStruct((2, slots, head_size), F32)] * heads,
        in_specs=[ANY, ANY],
        out_specs=[ANY] * heads,
        scratch_shapes=[pltpu.VMEM((heads, 2, slots, head_size), F32), pltpu.SemaphoreType.DMA((heads, 2, 2))],
        compiler_params=pltpu.CompilerParams(vmem_limit_bytes=PACK_LIMIT),
        cost_estimate=pl.CostEstimate(flops=8 << 30, bytes_accessed=8, transcendentals=0),
    )(keys, values)


def body(queries, cache_keys, cache_values, bounds):
    count = lax.axis_size("ctx")
    if count % 4:
        raise ValueError("ctx % 4")
    local_heads, slots, head_size = cache_keys.shape
    rows_t, query_heads = queries.shape[1:3]
    place = lax.axis_index("ctx").astype(jnp.int32)
    sizes = dict(
        rows_t=rows_t,
        group=query_heads // local_heads,
        head_size=head_size,
        slots=slots,
        total=slots * count,
    )
    heads = range(local_heads)
    heads = tuple(range(local_heads))
    scalars = (place.reshape(1), bounds.T)

    def step(jobs, pieces, sinks, fresh, final, *rest):
        names, call = make_step(jobs=jobs, pieces=pieces, sink=len(sinks), fresh=fresh, final=final, **sizes)
        taken = [got[n][h] for n in names for h in jobs] + [choice[h] for choice in sinks for h in jobs]
        if fresh:
            taken = [cache_keys, cache_values]
        return call(queries[0], *scalars, *taken, *rest)

    def send(arrays, source):
        moved = []
        for x in arrays:
            moved.append(exchange(x, source, count))
        return moved

    own = pack(cache_keys, cache_values)
    got = {"self": own}
    got["first"] = send(own, first_source)
    *flat, own_sinks = step(heads, ((("self", 0),) * 4,), (), True, 0)
    got["own_pair"] = send(own, pair_source)
    sinks = [own_sinks]
    if count == 8:
        far = send(sinks, lambda i: i ^ (4 if i % 2 else 2))
        near = send(far, pair_source)
        sink_args = (got["own_pair"], far[0], near[0], got["first"])
    else:
        have = 1
        while have <= count - SPAN:
            moved = send(sinks, lambda i, by=have: i - by)
            sinks = [jnp.where((place >= have) & (place < 2 * have), moved[0], sinks[0])]
            have *= 2
        sink_args = (sinks[0],)
    passed = []
    for h in heads:
        passed.append(pass_on(scalars[0], got["own_pair"][h], got["first"][h]))
    got["second"] = send(passed, second_source)
    got["first_pair"] = send(got["first"], pair_source)
    got["second_pair"] = send(got["second"], pair_source)
    for h in heads:
        here = slice(2 * h, 2 * h + 2)
        flat[here] = step((h,), PIECES[:1], (), False, 0, *flat[here])
    out = ()
    for h in heads:
        state, pieces = flat[2 * h : 2 * h + 2], PIECES[1:]
        if h < heads[-1]:
            state, pieces = step((h,), pieces[:1], (), False, 0, *state), pieces[1:]
        out = (step((h,), pieces, sink_args, False, 2 if h else 1, *state, *out),)
    return out[0][None]


def solution(mesh):
    placed = (P("ctx", None, "kvh", None), P("kvh", "ctx", None), P("kvh", "ctx", None), P())
    return jax.shard_map(body, mesh=mesh, in_specs=placed, out_specs=P("ctx", None, "kvh", None), check_vma=False)
```

profile of v0, /device:TPU:0, one launch (start us, length us, event | category | flops | bytes accessed | tf_op | source)
XLA Modules:
  0.0 53.6 jit_solution(8579343525579547687)
XLA Ops:
  0.0 0.0 copy-start.1
  0.0 0.0 copy-start
  0.0 2.1 %shard_map.46 = (f32[2,512,128]{2,1,0:T(8,128)}, f32[2,512,128]{2,1,0:T(8,128)}) custom-call(f32[2,512,128]{2,1,0:T(8,128)} %refs_3_.1, f32[2,512,128]{2,1,0:T(8,128)} %refs_4_.1), custom_call_target="tpu_custom_call" | custom-call | flops 8589934592 | bytes 8 | tf_op jit(solution)/shard_map/pallas_call | solution.py:298
  2.1 3.1 %collective-permute-start.8 = (f32[2,512,128]{2,1,0:T(8,128)}, f32[2,512,128]{2,1,0:T(8,128)S(1)}, u32[]{:S(2)}, u32[]{:S(2)}) collective-permute-start(f32[2,512,128]{2,1,0:T(8,128)} %get-tuple-element.24), channel_id=1, source_target_pairs={{16,0},{12,4},{4,8},{24,12},{0,16},{28,20},{20,24},{8,28},{17,1},{... | collective-permute-start | bytes 1572872 | tf_op jit(solution)/shard_map/ppermute | solution.py:34
  5.2 0.1 collective-permute-start.7
  5.3 1.5 %collective-permute-start = (f32[2,512,128]{2,1,0:T(8,128)}, f32[2,512,128]{2,1,0:T(8,128)}, u32[]{:S(2)}, u32[]{:S(2)}) collective-permute-start(f32[2,512,128]{2,1,0:T(8,128)} %get-tuple-element.18), channel_id=1, source_target_pairs={{16,0},{12,4},{4,8},{24,12},{0,16},{28,20},{20,24},{8,28},{17,1},{... | collective-permute-start | bytes 1572872 | tf_op jit(solution)/shard_map/ppermute | solution.py:34
  6.8 0.0 collective-permute-start.2
  6.8 0.0 copy-done.1
  6.8 0.0 copy-done
  6.8 0.0 copy-start.2
  6.8 1.0 %copy-done.2 = f32[2,512,128]{2,1,0:T(8,128)S(1)} copy-done((f32[2,512,128]{2,1,0:T(8,128)S(1)}, f32[2,512,128]{2,1,0:T(8,128)}, u32[]{:S(2)}) %copy-start.2) | copy-done | bytes 524312
  7.9 0.0 copy-start.3
  7.9 1.0 %copy-done.3 = f32[2,512,128]{2,1,0:T(8,128)S(1)} copy-done((f32[2,512,128]{2,1,0:T(8,128)S(1)}, f32[2,512,128]{2,1,0:T(8,128)}, u32[]{:S(2)}) %copy-start.3) | copy-done | bytes 524312
  8.9 6.0 %shard_map.48 = (f32[2048,128]{1,0:T(8,128)S(1)}, f32[2048,256]{1,0:T(8,128)S(1)}, f32[2048,128]{1,0:T(8,128)S(1)}, f32[2048,256]{1,0:T(8,128)S(1)}, f32[2,2,64,128]{3,2,1,0:T(8,128)S(1)}) custom-call(s32[1]{0:T(128)} %bitcast.place_ref.refs_0_, s32[3,8]{1,0:T(4,128)S(1)} %bitcast.18, f32[256,16,128]{2,1,0:T(8,128)S(1)} %bitcast.12, ...), custom_call_target="tpu_custom_call" | custom-call | flops 4294967296 | bytes 4194304 | tf_op jit(solution)/shard_map/pallas_call | solution.py:252
  14.9 0.7 %collective-permute-start.5 = (f32[2,2,64,128]{3,2,1,0:T(8,128)S(1)}, f32[2,2,64,128]{3,2,1,0:T(8,128)S(1)}, u32[]{:S(2)}, u32[]{:S(2)}) collective-permute-start(f32[2,2,64,128]{3,2,1,0:T(8,128)S(1)} %get-tuple-element.19), channel_id=1, source_target_pairs={{8,0},{20,4},{0,8},{28,12},{24,16},{4,20},{16,24},{12,28},{9,1},{2... | collective-permute-start | bytes 393224 | tf_op jit(solution)/shard_map/ppermute | solution.py:34
  15.6 0.0 collective-permute-done.8.came_ref.refs_4_.refs_8_
  15.6 0.0 collective-permute-done.7.pair_ref.refs_3_.refs_5_
  15.6 0.1 shard_map.50
  15.7 0.7 %collective-permute-start.9 = (f32[2,512,128]{2,1,0:T(8,128)S(1)}, f32[2,512,128]{2,1,0:T(8,128)S(1)}, u32[]{:S(2)}, u32[]{:S(2)}) collective-permute-start(f32[2,512,128]{2,1,0:T(8,128)S(1)} %shard_map.50), channel_id=1, source_target_pairs={{12,0},{20,4},{24,8},{0,12},{28,16},{4,20},{8,24},{16,28},{13,1},{... | collective-permute-start | bytes 1572872 | tf_op jit(solution)/shard_map/ppermute | solution.py:34
  16.4 4.7 %collective-permute-done.5 = f32[2,2,64,128]{3,2,1,0:T(8,128)S(1)} collective-permute-done((f32[2,2,64,128]{3,2,1,0:T(8,128)S(1)}, f32[2,2,64,128]{3,2,1,0:T(8,128)S(1)}, u32[]{:S(2)}, u32[]{:S(2)}) %collective-permute-start.5) | collective-permute-done | bytes 131104 | tf_op jit(solution)/shard_map/ppermute | solution.py:34
  21.1 0.0 collective-permute-start.6
  21.1 0.0 collective-permute-done.came_ref.refs_4_.refs_9_
  21.1 0.0 collective-permute-done.2.pair_ref.refs_3_.refs_6_
  21.1 1.3 %shard_map.47 = f32[2,512,128]{2,1,0:T(8,128)S(1)} custom-call(s32[1]{0:T(128)} %bitcast.place_ref.refs_0_, f32[2,512,128]{2,1,0:T(8,128)} %collective-permute-done.2.pair_ref.refs_3_.refs_6_, f32[2,512,128]{2,1,0:T(8,128)} %collective-permute-done.came_ref.refs_4_.refs_9_), custom_call_target="tpu_custom_call" | custom-call | bytes 2097152 | tf_op jit(solution)/shard_map/pallas_call | solution.py:272
  22.4 0.1 collective-permute-start.3
  22.5 0.6 %collective-permute-start.11 = (f32[2,512,128]{2,1,0:T(8,128)S(1)}, f32[2,512,128]{2,1,0:T(8,128)S(1)}, u32[]{:S(2)}, u32[]{:S(2)}) collective-permute-start(f32[2,512,128]{2,1,0:T(8,128)S(1)} %collective-permute-done.8.came_ref.refs_4_.refs_8_), channel_id=1, source_target_pairs={{4,0},{0,4},{12,8},{8,12},{20,16},{16,20},{28,24},{24,28},{5,1},{1... | collective-permute-start | bytes 1572872 | tf_op jit(solution)/shard_map/ppermute | solution.py:34
  23.1 0.0 collective-permute-done.6
  23.1 0.1 collective-permute-start.1
  23.2 2.4 %collective-permute-done.9.refs_4_.refs_3_ = f32[2,512,128]{2,1,0:T(8,128)S(1)} collective-permute-done((f32[2,512,128]{2,1,0:T(8,128)S(1)}, f32[2,512,128]{2,1,0:T(8,128)S(1)}, u32[]{:S(2)}, u32[]{:S(2)}) %collective-permute-start.9) | collective-permute-done | bytes 524320 | tf_op jit(solution)/shard_map/ppermute | solution.py:34
  25.5 0.0 collective-permute-start.10
  25.6 3.4 %shard_map.51 = (f32[2048,128]{1,0:T(8,128)S(1)}, f32[2048,256]{1,0:T(8,128)S(1)}) custom-call(s32[1]{0:T(128)} %bitcast.place_ref.refs_0_, s32[3,8]{1,0:T(4,128)S(1)} %bitcast.19, f32[256,16,128]{2,1,0:T(8,128)S(1)} %bitcast.13, f32[2,512,128]{2,1,0:T(8,128)S(1)} %collective-permute-done.7.pair_ref.refs_3_.refs_5_, ...), custom_call_target="tpu_custom_call" | custom-call | flops 2147483648 | bytes 4194304 | tf_op jit(solution)/shard_map/pallas_call | solution.py:252
  29.0 2.2 %collective-permute-done.3.refs_4_ = f32[2,512,128]{2,1,0:T(8,128)S(1)} collective-permute-done((f32[2,512,128]{2,1,0:T(8,128)S(1)}, f32[2,512,128]{2,1,0:T(8,128)S(1)}, u32[]{:S(2)}, u32[]{:S(2)}) %collective-permute-start.3) | collective-permute-done | bytes 524320 | tf_op jit(solution)/shard_map/ppermute | solution.py:34
  31.2 0.1 collective-permute-start.4
  31.3 4.1 %shard_map.49 = (f32[2048,128]{1,0:T(8,128)S(1)}, f32[2048,256]{1,0:T(8,128)S(1)}) custom-call(s32[1]{0:T(128)} %bitcast.place_ref.refs_0_, s32[3,8]{1,0:T(4,128)S(1)} %bitcast.20, f32[256,16,128]{2,1,0:T(8,128)S(1)} %bitcast.14, f32[2,512,128]{2,1,0:T(8,128)} %collective-permute-done.2.pair_ref.refs_3_.refs_6_, ...), custom_call_target="tpu_custom_call" | custom-call | flops 2147483648 | bytes 4194304 | tf_op jit(solution)/shard_map/pallas_call | solution.py:252
  35.4 0.0 collective-permute-done.11.refs_3_
  35.4 3.6 %shard_map.52 = (f32[2048,128]{1,0:T(8,128)S(1)}, f32[2048,256]{1,0:T(8,128)S(1)}) custom-call(s32[1]{0:T(128)} %bitcast.place_ref.refs_0_, s32[3,8]{1,0:T(4,128)S(1)} %bitcast.21, f32[256,16,128]{2,1,0:T(8,128)S(1)} %bitcast.15, f32[2,512,128]{2,1,0:T(8,128)S(1)} %collective-permute-done.11.refs_3_, ...), custom_call_target="tpu_custom_call" | custom-call | flops 2147483648 | bytes 4194304 | tf_op jit(solution)/shard_map/pallas_call | solution.py:252
  39.0 0.0 collective-permute-done.10.refs_4_
  39.1 5.7 %shard_map.53.refs_12_ = f32[256,16,128]{2,1,0:T(8,128)} custom-call(s32[1]{0:T(128)} %bitcast.place_ref.refs_0_, s32[3,8]{1,0:T(4,128)S(1)} %bitcast.22, f32[256,16,128]{2,1,0:T(8,128)S(1)} %bitcast.16, f32[2,512,128]{2,1,0:T(8,128)S(1)} %collective-permute-done.9.refs_4_.refs_3_, f32[2,512,128]{2,1,0:T(8,128)S(1)} %collective-permute-done.10.refs_4_, ...), custom_call_target="tpu_custom_call" | custom-call | flops 2147483648 | bytes 4194304 | tf_op jit(solution)/shard_map/pallas_call | solution.py:252
  44.8 0.0 collective-permute-done.1.refs_3_
  44.8 0.0 collective-permute-done.4.refs_5_
  44.8 8.6 %shard_map.54 = f32[256,16,128]{2,1,0:T(8,128)} custom-call(s32[1]{0:T(128)} %bitcast.place_ref.refs_0_, s32[3,8]{1,0:T(4,128)S(1)} %bitcast.23, f32[256,16,128]{2,1,0:T(8,128)S(1)} %bitcast.17, f32[2,512,128]{2,1,0:T(8,128)S(1)} %collective-permute-done.1.refs_3_, ...), custom_call_target="tpu_custom_call", output_to_operand_aliasing={{}: (12, {})} | custom-call | flops 4294967296 | bytes 4194304 | tf_op jit(solution)/shard_map/pallas_call | solution.py:252
  (2 shorter events, 0.0 us)
Async XLA Ops:
  0.0 6.8 %copy-start.1 = (s32[8,3]{0,1:T(4,128)S(1)}, s32[8,3]{0,1:T(4,128)}, u32[]{:S(2)}) copy-start(s32[8,3]{0,1:T(4,128)} %param.7) | copy-start | bytes 292
  0.0 6.8 %copy-start = (f32[1,256,16,128]{3,2,1,0:T(8,128)S(1)}, f32[1,256,16,128]{3,2,1,0:T(8,128)}, u32[]{:S(2)}) copy-start(f32[1,256,16,128]{3,2,1,0:T(8,128)} %param.4) | copy-start | bytes 6291460
  2.1 13.5 %collective-permute-start.8 = (f32[2,512,128]{2,1,0:T(8,128)}, f32[2,512,128]{2,1,0:T(8,128)S(1)}, u32[]{:S(2)}, u32[]{:S(2)}) collective-permute-start(f32[2,512,128]{2,1,0:T(8,128)} %get-tuple-element.24), channel_id=1, source_target_pairs={{16,0},{12,4},{4,8},{24,12},{0,16},{28,20},{20,24},{8,28},{17,1},{... | collective-permute-start | bytes 1572872 | tf_op jit(solution)/shard_map/ppermute | solution.py:34
  5.2 10.4 %collective-permute-start.7 = (f32[2,512,128]{2,1,0:T(8,128)}, f32[2,512,128]{2,1,0:T(8,128)S(1)}, u32[]{:S(2)}, u32[]{:S(2)}) collective-permute-start(f32[2,512,128]{2,1,0:T(8,128)} %get-tuple-element.24), channel_id=1, source_target_pairs={{4,0},{0,4},{12,8},{8,12},{20,16},{16,20},{28,24},{24,28},{5,1},{1... | collective-permute-start | bytes 1572872 | tf_op jit(solution)/shard_map/ppermute | solution.py:34
  5.3 15.9 %collective-permute-start = (f32[2,512,128]{2,1,0:T(8,128)}, f32[2,512,128]{2,1,0:T(8,128)}, u32[]{:S(2)}, u32[]{:S(2)}) collective-permute-start(f32[2,512,128]{2,1,0:T(8,128)} %get-tuple-element.18), channel_id=1, source_target_pairs={{16,0},{12,4},{4,8},{24,12},{0,16},{28,20},{20,24},{8,28},{17,1},{... | collective-permute-start | bytes 1572872 | tf_op jit(solution)/shard_map/ppermute | solution.py:34
  6.8 14.3 %collective-permute-start.2 = (f32[2,512,128]{2,1,0:T(8,128)}, f32[2,512,128]{2,1,0:T(8,128)}, u32[]{:S(2)}, u32[]{:S(2)}) collective-permute-start(f32[2,512,128]{2,1,0:T(8,128)} %get-tuple-element.18), channel_id=1, source_target_pairs={{4,0},{0,4},{12,8},{8,12},{20,16},{16,20},{28,24},{24,28},{5,1},{1... | collective-permute-start | bytes 1572872 | tf_op jit(solution)/shard_map/ppermute | solution.py:34
  6.8 1.0 %copy-start.2 = (f32[2,512,128]{2,1,0:T(8,128)S(1)}, f32[2,512,128]{2,1,0:T(8,128)}, u32[]{:S(2)}) copy-start(f32[2,512,128]{2,1,0:T(8,128)} %refs_3_.1) | copy-start | bytes 1572868
  7.9 1.0 %copy-start.3 = (f32[2,512,128]{2,1,0:T(8,128)S(1)}, f32[2,512,128]{2,1,0:T(8,128)}, u32[]{:S(2)}) copy-start(f32[2,512,128]{2,1,0:T(8,128)} %refs_4_.1) | copy-start | bytes 1572868
  14.9 6.2 %collective-permute-start.5 = (f32[2,2,64,128]{3,2,1,0:T(8,128)S(1)}, f32[2,2,64,128]{3,2,1,0:T(8,128)S(1)}, u32[]{:S(2)}, u32[]{:S(2)}) collective-permute-start(f32[2,2,64,128]{3,2,1,0:T(8,128)S(1)} %get-tuple-element.19), channel_id=1, source_target_pairs={{8,0},{20,4},{0,8},{28,12},{24,16},{4,20},{16,24},{12,28},{9,1},{2... | collective-permute-start | bytes 393224 | tf_op jit(solution)/shard_map/ppermute | solution.py:34
  15.7 9.9 %collective-permute-start.9 = (f32[2,512,128]{2,1,0:T(8,128)S(1)}, f32[2,512,128]{2,1,0:T(8,128)S(1)}, u32[]{:S(2)}, u32[]{:S(2)}) collective-permute-start(f32[2,512,128]{2,1,0:T(8,128)S(1)} %shard_map.50), channel_id=1, source_target_pairs={{12,0},{20,4},{24,8},{0,12},{28,16},{4,20},{8,24},{16,28},{13,1},{... | collective-permute-start | bytes 1572872 | tf_op jit(solution)/shard_map/ppermute | solution.py:34
  21.1 1.9 %collective-permute-start.6 = (f32[2,2,64,128]{3,2,1,0:T(8,128)S(1)}, f32[2,2,64,128]{3,2,1,0:T(8,128)S(1)}, u32[]{:S(2)}, u32[]{:S(2)}) collective-permute-start(f32[2,2,64,128]{3,2,1,0:T(8,128)S(1)} %collective-permute-done.5), channel_id=1, source_target_pairs={{4,0},{0,4},{12,8},{8,12},{20,16},{16,20},{28,24},{24,28},{5,1},{1... | collective-permute-start | bytes 393224 | tf_op jit(solution)/shard_map/ppermute | solution.py:34
  22.4 8.8 %collective-permute-start.3 = (f32[2,512,128]{2,1,0:T(8,128)S(1)}, f32[2,512,128]{2,1,0:T(8,128)S(1)}, u32[]{:S(2)}, u32[]{:S(2)}) collective-permute-start(f32[2,512,128]{2,1,0:T(8,128)S(1)} %shard_map.47), channel_id=1, source_target_pairs={{12,0},{20,4},{24,8},{0,12},{28,16},{4,20},{8,24},{16,28},{13,1},{... | collective-permute-start | bytes 1572872 | tf_op jit(solution)/shard_map/ppermute | solution.py:34
  22.5 12.9 %collective-permute-start.11 = (f32[2,512,128]{2,1,0:T(8,128)S(1)}, f32[2,512,128]{2,1,0:T(8,128)S(1)}, u32[]{:S(2)}, u32[]{:S(2)}) collective-permute-start(f32[2,512,128]{2,1,0:T(8,128)S(1)} %collective-permute-done.8.came_ref.refs_4_.refs_8_), channel_id=1, source_target_pairs={{4,0},{0,4},{12,8},{8,12},{20,16},{16,20},{28,24},{24,28},{5,1},{1... | collective-permute-start | bytes 1572872 | tf_op jit(solution)/shard_map/ppermute | solution.py:34
  23.1 21.7 %collective-permute-start.1 = (f32[2,512,128]{2,1,0:T(8,128)}, f32[2,512,128]{2,1,0:T(8,128)S(1)}, u32[]{:S(2)}, u32[]{:S(2)}) collective-permute-start(f32[2,512,128]{2,1,0:T(8,128)} %collective-permute-done.came_ref.refs_4_.refs_9_), channel_id=1, source_target_pairs={{4,0},{0,4},{12,8},{8,12},{20,16},{16,20},{28,24},{24,28},{5,1},{1... | collective-permute-start | bytes 1572872 | tf_op jit(solution)/shard_map/ppermute | solution.py:34
  25.5 13.5 %collective-permute-start.10 = (f32[2,512,128]{2,1,0:T(8,128)S(1)}, f32[2,512,128]{2,1,0:T(8,128)S(1)}, u32[]{:S(2)}, u32[]{:S(2)}) collective-permute-start(f32[2,512,128]{2,1,0:T(8,128)S(1)} %collective-permute-done.9.refs_4_.refs_3_), channel_id=1, source_target_pairs={{4,0},{0,4},{12,8},{8,12},{20,16},{16,20},{28,24},{24,28},{5,1},{1... | collective-permute-start | bytes 1572872 | tf_op jit(solution)/shard_map/ppermute | solution.py:34
  31.2 13.6 %collective-permute-start.4 = (f32[2,512,128]{2,1,0:T(8,128)S(1)}, f32[2,512,128]{2,1,0:T(8,128)S(1)}, u32[]{:S(2)}, u32[]{:S(2)}) collective-permute-start(f32[2,512,128]{2,1,0:T(8,128)S(1)} %collective-permute-done.3.refs_4_), channel_id=1, source_target_pairs={{4,0},{0,4},{12,8},{8,12},{20,16},{16,20},{28,24},{24,28},{5,1},{1... | collective-permute-start | bytes 1572872 | tf_op jit(solution)/shard_map/ppermute | solution.py:34
where the time goes:
time: 53.9 us; the launch traced here: 53.6 us
  Pallas kernels  35 us (65%)
  waiting for transfers between devices  9.3 us (17%)
  starting transfers between devices  6.93 us (13%)
  local copies, waits for them, and re-layouts  2.11 us (4%)
    pallas_call x6, Pallas kernels, call(): pl.pallas_call(kernel, out_shape=out_shape, in_specs=in_specs, out_specs=...  31.5 us
    ppermute x12, waiting for transfers between devices, exchange(): lax.ppermute(x, 'ctx', [(source(i) % count, i) for i in range(count)])  9.3 us
    ppermute x12, starting transfers between devices, exchange(): lax.ppermute(x, 'ctx', [(source(i) % count, i) for i in range(count)])  6.93 us
    pallas_call x1, Pallas kernels, pack(): pl.pallas_call(kernel, out_shape=[jax.ShapeDtypeStruct((2, slots, head_si...  2.13 us
    unnamed x8, local copies, waits for them, and re-layouts  2.09 us
    pallas_call x2, Pallas kernels, pass_on(): pl.pallas_call(kernel, out_shape=jax.ShapeDtypeStruct(came.shape, F32), i...  1.31 us
  transfers between devices with their start and end apart: 12, of which 3 were waited for; matrix products, arithmetic and copies ran while one was open for 0% of the time, Pallas kernels for 45%

commit v1 on v0

--- a/solution.py
+++ b/solution.py
@@ -12,6 +12,7 @@
 SPAN = 4
 LANES = 128
 BLOCK_ROWS = 1024
+OUT_PARTS = 8
 VMEM_LIMIT = 20 << 20
 PACK_LIMIT = 58 << 20
 NEG = -1e30
@@ -78,7 +79,7 @@
             return front
 
         place_ref, bounds_ref, q_ref = take(3)
-        sources = {n: take(2 if fresh else count) for n in names}
+        sources = {n: take(count) for n in names}
 
         def source(job, name, j):
             return sources[name][job][j]
@@ -95,18 +96,6 @@
         k_cat, v_cat = take(2)
         ks_cat, vs_cat = take(2) if sink else (None, None)
         o_buf, o_sem = take(2) if final else (None, None)
-        loads = {}
-        if fresh:
-            kv_buf, sems = take(2)
-            for job, head in enumerate(jobs):
-                loads[job] = [
-                    pltpu.make_async_copy(ref.at[head], kv_buf.at[job, j], sems.at[job, j])
-                    for j, ref in enumerate(sources["self"])
-                ]
-                for copy in loads[job]:
-                    copy.start()
-            sources = {"self": [kv_buf.at[job] for job in range(count)]}
-
         place = place_ref[0]
         role = lax.rem(place, 4)
         first, lower, upper = (bounds_ref[j, place] for j in range(3))
@@ -170,8 +159,6 @@
 
         copies = []
         for job, head in enumerate(jobs):
-            for copy in loads.get(job, ()):
-                copy.wait()
             if fresh:
                 for j in range(2):
                     sink_out[job, j] = source(job, "self", j)[:SINK]
@@ -209,14 +196,18 @@
                     mixed = mixed + states_in[job][0][here] * shrink
                 if final:
                     sums = jnp.sum(sums, axis=1, keepdims=True)
-                    o_buf[chunk] = (mixed / sums).reshape(block_t, group, head_size)
-                    copy = pltpu.make_async_copy(
-                        o_buf.at[chunk],
-                        out_ref.at[pl.ds(chunk * block_t, block_t), pl.ds(head * group, group)],
-                        o_sem.at[chunk],
-                    )
-                    copy.start()
-                    copies.append(copy)
+                    part_t = block_t // OUT_PARTS
+                    for part in range(OUT_PARTS):
+                        rows_of = slice(part * part_t * group, (part + 1) * part_t * group)
+                        value = mixed[rows_of] / sums[rows_of]
+                        o_buf[chunk, part] = value.reshape(part_t, group, head_size)
+                        copy = pltpu.make_async_copy(
+                            o_buf.at[chunk, part],
+                            out_ref.at[pl.ds(chunk * block_t + part * part_t, part_t), pl.ds(head * group, group)],
+                            o_sem.at[chunk, part],
+                        )
+                        copy.start()
+                        copies.append(copy)
                 else:
                     acc_out, stat_out = states_out[job]
                     acc_out[here] = mixed
@@ -225,17 +216,15 @@
         for copy in copies:
             copy.wait()
 
-    taken = 2 if fresh else len(names) * count + count * sink + 2 * count
-    in_specs = [SMEM, SMEM, VMEM] + [ANY if fresh else VMEM] * taken
+    taken = len(names) * count + count * sink + 2 * count * (not fresh)
+    in_specs = [SMEM, SMEM, VMEM] + [VMEM] * taken
     in_specs += [ANY] * (final == 2)
     scratch = [pltpu.VMEM((count, width, 4 * LANES), BF16), pltpu.VMEM((count, width, 2 * LANES), BF16)]
     if sink:
         scratch += [pltpu.VMEM((count, 2 * SINK, n * LANES), BF16) for n in (4, 2)]
     if final:
-        scratch += [pltpu.VMEM((chunks, block_t, group, head_size), F32), pltpu.SemaphoreType.DMA((chunks,))]
-
-    if fresh:
-        scratch += [pltpu.VMEM((count, 2, slots, head_size), F32), pltpu.SemaphoreType.DMA((count, 2))]
+        shape = (chunks, OUT_PARTS, block_t // OUT_PARTS, group, head_size)
+        scratch += [pltpu.VMEM(shape, F32), pltpu.SemaphoreType.DMA((chunks, OUT_PARTS))]
 
     def call(queries, *args):
         if final:
@@ -327,8 +316,6 @@
     def step(jobs, pieces, sinks, fresh, final, *rest):
         names, call = make_step(jobs=jobs, pieces=pieces, sink=len(sinks), fresh=fresh, final=final, **sizes)
         taken = [got[n][h] for n in names for h in jobs] + [choice[h] for choice in sinks for h in jobs]
-        if fresh:
-            taken = [cache_keys, cache_values]
         return call(queries[0], *scalars, *taken, *rest)
 
     def send(arrays, source):
@@ -367,8 +354,9 @@
     for h in heads:
         state, pieces = flat[2 * h : 2 * h + 2], PIECES[1:]
         if h < heads[-1]:
-            state, pieces = step((h,), pieces[:1], (), False, 0, *state), pieces[1:]
-        out = (step((h,), pieces, sink_args, False, 2 if h else 1, *state, *out),)
+            state, pieces = step((h,), pieces[:1], sink_args, False, 0, *state), pieces[1:]
+        late = () if h < heads[-1] else sink_args
+        out = (step((h,), pieces, late, False, 2 if h else 1, *state, *out),)
     return out[0][None]
 
 

time: 53.9 us -> 52.7 us (0.978)
  waiting for transfers between devices: 9.3 us -> 7.23 us
  starting transfers between devices: 6.93 us -> 8.33 us
  Pallas kernels: 35 us -> 34.4 us
    ppermute x12, waiting for transfers between devices: 9.3 us -> 7.23 us  [exchange(): lax.ppermute(x, 'ctx', [(source(i) % count, i) for i in range(count)])]
    ppermute x12, starting transfers between devices: 6.93 us -> 8.33 us  [exchange(): lax.ppermute(x, 'ctx', [(source(i) % count, i) for i in range(count)])]
    pallas_call x6, Pallas kernels: 31.5 us -> 31 us  [call(): pl.pallas_call(kernel, out_shape=out_shape, in_specs=in_specs, out_specs=...]
  transfers between devices with their start and end apart: 12 -> 12, of which waited for: 3 -> 4; matrix products, arithmetic and copies ran while one was open for 0% -> 0% of each run, Pallas kernels for 45% -> 46%
where the time goes in v1:
time: 52.7 us; the launch traced here: 52.4 us
  Pallas kernels  34.4 us (65%)
  starting transfers between devices  8.33 us (16%)
  waiting for transfers between devices  7.23 us (14%)
  local copies, waits for them, and re-layouts  2.13 us (4%)
    pallas_call x6, Pallas kernels, call(): pl.pallas_call(kernel, out_shape=out_shape, in_specs=in_specs, out_specs=...  31 us
    ppermute x12, starting transfers between devices, exchange(): lax.ppermute(x, 'ctx', [(source(i) % count, i) for i in range(count)])  8.33 us
    ppermute x12, waiting for transfers between devices, exchange(): lax.ppermute(x, 'ctx', [(source(i) % count, i) for i in range(count)])  7.23 us
    pallas_call x1, Pallas kernels, pack(): pl.pallas_call(kernel, out_shape=[jax.ShapeDtypeStruct((2, slots, head_si...  2.13 us
    unnamed x8, local copies, waits for them, and re-layouts  2.1 us
    pallas_call x2, Pallas kernels, pass_on(): pl.pallas_call(kernel, out_shape=jax.ShapeDtypeStruct(came.shape, F32), i...  1.31 us
  transfers between devices with their start and end apart: 12, of which 4 were waited for; matrix products, arithmetic and copies ran while one was open for 0% of the time, Pallas kernels for 46%

profile of v1, /device:TPU:0, one launch (start us, length us, event | category | flops | bytes accessed | tf_op | source)
XLA Modules:
  0.0 52.4 jit_solution(6629352387606353159)
XLA Ops:
  0.0 0.0 copy-start.1
  0.0 0.0 copy-start
  0.0 2.1 %shard_map.46 = (f32[2,512,128]{2,1,0:T(8,128)}, f32[2,512,128]{2,1,0:T(8,128)}) custom-call(f32[2,512,128]{2,1,0:T(8,128)} %k_ref.1, f32[2,512,128]{2,1,0:T(8,128)} %v_ref.1), custom_call_target="tpu_custom_call" | custom-call | flops 8589934592 | bytes 8 | tf_op jit(solution)/shard_map/pallas_call | solution.py:287
  2.1 3.1 %collective-permute-start.8 = (f32[2,512,128]{2,1,0:T(8,128)}, f32[2,512,128]{2,1,0:T(8,128)}, u32[]{:S(2)}, u32[]{:S(2)}) collective-permute-start(f32[2,512,128]{2,1,0:T(8,128)} %get-tuple-element.19.refs_3_), channel_id=1, source_target_pairs={{16,0},{12,4},{4,8},{24,12},{0,16},{28,20},{20,24},{8,28},{17,1},{... | collective-permute-start | bytes 1572872 | tf_op jit(solution)/shard_map/ppermute | solution.py:35
  5.2 0.1 collective-permute-start.7
  5.3 1.5 %collective-permute-start = (f32[2,512,128]{2,1,0:T(8,128)}, f32[2,512,128]{2,1,0:T(8,128)S(1)}, u32[]{:S(2)}, u32[]{:S(2)}) collective-permute-start(f32[2,512,128]{2,1,0:T(8,128)} %get-tuple-element.18.refs_4_), channel_id=1, source_target_pairs={{16,0},{12,4},{4,8},{24,12},{0,16},{28,20},{20,24},{8,28},{17,1},{... | collective-permute-start | bytes 1572872 | tf_op jit(solution)/shard_map/ppermute | solution.py:35
  6.8 0.0 collective-permute-start.2
  6.8 0.0 copy-done.1
  6.8 0.0 copy-done
  6.8 0.0 copy-start.2
  6.8 1.1 %copy-done.2 = f32[2,512,128]{2,1,0:T(8,128)S(1)} copy-done((f32[2,512,128]{2,1,0:T(8,128)S(1)}, f32[2,512,128]{2,1,0:T(8,128)}, u32[]{:S(2)}) %copy-start.2) | copy-done | bytes 524312
  7.9 0.0 copy-start.3
  7.9 1.0 %copy-done.3 = f32[2,512,128]{2,1,0:T(8,128)S(1)} copy-done((f32[2,512,128]{2,1,0:T(8,128)S(1)}, f32[2,512,128]{2,1,0:T(8,128)}, u32[]{:S(2)}) %copy-start.3) | copy-done | bytes 524312
  8.9 5.6 %shard_map.48 = (f32[2048,128]{1,0:T(8,128)S(1)}, f32[2048,256]{1,0:T(8,128)S(1)}, f32[2048,128]{1,0:T(8,128)S(1)}, f32[2048,256]{1,0:T(8,128)S(1)}, f32[2,2,64,128]{3,2,1,0:T(8,128)S(1)}) custom-call(s32[1]{0:T(128)} %bitcast.place_ref.refs_0_, s32[3,8]{1,0:T(4,128)S(1)} %bitcast.18, f32[256,16,128]{2,1,0:T(8,128)S(1)} %bitcast.12, ...), custom_call_target="tpu_custom_call" | custom-call | flops 4294967296 | bytes 4194304 | tf_op jit(solution)/shard_map/pallas_call | solution.py:241
  14.6 0.7 %collective-permute-start.5 = (f32[2,2,64,128]{3,2,1,0:T(8,128)S(1)}, f32[2,2,64,128]{3,2,1,0:T(8,128)S(1)}, u32[]{:S(2)}, u32[]{:S(2)}) collective-permute-start(f32[2,2,64,128]{3,2,1,0:T(8,128)S(1)} %get-tuple-element.20), channel_id=1, source_target_pairs={{8,0},{20,4},{0,8},{28,12},{24,16},{4,20},{16,24},{12,28},{9,1},{2... | collective-permute-start | bytes 393224 | tf_op jit(solution)/shard_map/ppermute | solution.py:35
  15.3 0.0 collective-permute-done.8.came_ref.refs_4_.refs_8_
  15.3 0.0 collective-permute-done.7.pair_ref.refs_3_.refs_5_
  15.3 1.3 %shard_map.50 = f32[2,512,128]{2,1,0:T(8,128)S(1)} custom-call(s32[1]{0:T(128)} %bitcast.place_ref.refs_0_, f32[2,512,128]{2,1,0:T(8,128)} %collective-permute-done.7.pair_ref.refs_3_.refs_5_, f32[2,512,128]{2,1,0:T(8,128)} %collective-permute-done.8.came_ref.refs_4_.refs_8_), custom_call_target="tpu_custom_call" | custom-call | bytes 2097152 | tf_op jit(solution)/shard_map/pallas_call | solution.py:261
  16.5 0.7 %collective-permute-start.9 = (f32[2,512,128]{2,1,0:T(8,128)S(1)}, f32[2,512,128]{2,1,0:T(8,128)S(1)}, u32[]{:S(2)}, u32[]{:S(2)}) collective-permute-start(f32[2,512,128]{2,1,0:T(8,128)S(1)} %shard_map.50), channel_id=1, source_target_pairs={{12,0},{20,4},{24,8},{0,12},{28,16},{4,20},{8,24},{16,28},{13,1},{... | collective-permute-start | bytes 1572872 | tf_op jit(solution)/shard_map/ppermute | solution.py:35
  17.2 2.4 %collective-permute-done.5 = f32[2,2,64,128]{3,2,1,0:T(8,128)S(1)} collective-permute-done((f32[2,2,64,128]{3,2,1,0:T(8,128)S(1)}, f32[2,2,64,128]{3,2,1,0:T(8,128)S(1)}, u32[]{:S(2)}, u32[]{:S(2)}) %collective-permute-start.5) | collective-permute-done | bytes 131104 | tf_op jit(solution)/shard_map/ppermute | solution.py:35
  19.6 0.1 collective-permute-start.6
  19.7 0.1 collective-permute-done.came_ref.refs_4_.refs_9_
  19.8 0.0 collective-permute-done.2.pair_ref.refs_3_.refs_6_
  19.8 0.1 shard_map.47
  19.9 1.4 %collective-permute-start.3 = (f32[2,512,128]{2,1,0:T(8,128)S(1)}, f32[2,512,128]{2,1,0:T(8,128)S(1)}, u32[]{:S(2)}, u32[]{:S(2)}) collective-permute-start(f32[2,512,128]{2,1,0:T(8,128)S(1)} %shard_map.47), channel_id=1, source_target_pairs={{12,0},{20,4},{24,8},{0,12},{28,16},{4,20},{8,24},{16,28},{13,1},{... | collective-permute-start | bytes 1572872 | tf_op jit(solution)/shard_map/ppermute | solution.py:35
  21.3 0.1 collective-permute-start.11
  21.3 0.0 collective-permute-done.6
  21.4 0.6 %collective-permute-start.1 = (f32[2,512,128]{2,1,0:T(8,128)S(1)}, f32[2,512,128]{2,1,0:T(8,128)S(1)}, u32[]{:S(2)}, u32[]{:S(2)}) collective-permute-start(f32[2,512,128]{2,1,0:T(8,128)S(1)} %collective-permute-done.came_ref.refs_4_.refs_9_), channel_id=1, source_target_pairs={{4,0},{0,4},{12,8},{8,12},{20,16},{16,20},{28,24},{24,28},{5,1},{1... | collective-permute-start | bytes 1572872 | tf_op jit(solution)/shard_map/ppermute | solution.py:35
  21.9 3.3 %collective-permute-done.9.refs_4_.refs_3_ = f32[2,512,128]{2,1,0:T(8,128)S(1)} collective-permute-done((f32[2,512,128]{2,1,0:T(8,128)S(1)}, f32[2,512,128]{2,1,0:T(8,128)S(1)}, u32[]{:S(2)}, u32[]{:S(2)}) %collective-permute-start.9) | collective-permute-done | bytes 524320 | tf_op jit(solution)/shard_map/ppermute | solution.py:35
  25.2 0.1 collective-permute-start.10
  25.3 4.1 %shard_map.51 = (f32[2048,128]{1,0:T(8,128)S(1)}, f32[2048,256]{1,0:T(8,128)S(1)}) custom-call(s32[1]{0:T(128)} %bitcast.place_ref.refs_0_, s32[3,8]{1,0:T(4,128)S(1)} %bitcast.19, f32[256,16,128]{2,1,0:T(8,128)S(1)} %bitcast.13, f32[2,512,128]{2,1,0:T(8,128)} %collective-permute-done.7.pair_ref.refs_3_.refs_5_, ...), custom_call_target="tpu_custom_call" | custom-call | flops 2147483648 | bytes 4194304 | tf_op jit(solution)/shard_map/pallas_call | solution.py:241
  29.4 1.4 %collective-permute-done.3.refs_4_ = f32[2,512,128]{2,1,0:T(8,128)S(1)} collective-permute-done((f32[2,512,128]{2,1,0:T(8,128)S(1)}, f32[2,512,128]{2,1,0:T(8,128)S(1)}, u32[]{:S(2)}, u32[]{:S(2)}) %collective-permute-start.3) | collective-permute-done | bytes 524320 | tf_op jit(solution)/shard_map/ppermute | solution.py:35
  30.8 0.1 collective-permute-start.4
  30.9 3.4 %shard_map.49 = (f32[2048,128]{1,0:T(8,128)S(1)}, f32[2048,256]{1,0:T(8,128)S(1)}) custom-call(s32[1]{0:T(128)} %bitcast.place_ref.refs_0_, s32[3,8]{1,0:T(4,128)S(1)} %bitcast.20, f32[256,16,128]{2,1,0:T(8,128)S(1)} %bitcast.14, f32[2,512,128]{2,1,0:T(8,128)S(1)} %collective-permute-done.2.pair_ref.refs_3_.refs_6_, ...), custom_call_target="tpu_custom_call" | custom-call | flops 2147483648 | bytes 4194304 | tf_op jit(solution)/shard_map/pallas_call | solution.py:241
  34.4 0.0 collective-permute-done.11.refs_3_
  34.4 5.6 %shard_map.52 = (f32[2048,128]{1,0:T(8,128)S(1)}, f32[2048,256]{1,0:T(8,128)S(1)}) custom-call(s32[1]{0:T(128)} %bitcast.place_ref.refs_0_, s32[3,8]{1,0:T(4,128)S(1)} %bitcast.21, f32[256,16,128]{2,1,0:T(8,128)S(1)} %bitcast.15, f32[2,512,128]{2,1,0:T(8,128)S(1)} %collective-permute-done.11.refs_3_, ...), custom_call_target="tpu_custom_call" | custom-call | flops 2147483648 | bytes 4194304 | tf_op jit(solution)/shard_map/pallas_call | solution.py:241
  40.0 0.0 collective-permute-done.10.refs_4_
  40.0 4.2 %shard_map.53.refs_12_ = f32[256,16,128]{2,1,0:T(8,128)} custom-call(s32[1]{0:T(128)} %bitcast.place_ref.refs_0_, s32[3,8]{1,0:T(4,128)S(1)} %bitcast.22, f32[256,16,128]{2,1,0:T(8,128)S(1)} %bitcast.16, f32[2,512,128]{2,1,0:T(8,128)S(1)} %collective-permute-done.9.refs_4_.refs_3_, f32[2,512,128]{2,1,0:T(8,128)S(1)} %collective-permute-done.10.refs_4_, ...), custom_call_target="tpu_custom_call" | custom-call | flops 2147483648 | bytes 4194304 | tf_op jit(solution)/shard_map/pallas_call | solution.py:241
  44.3 0.0 collective-permute-done.1.refs_3_
  44.3 0.0 collective-permute-done.4.refs_5_
  44.3 8.0 %shard_map.54 = f32[256,16,128]{2,1,0:T(8,128)} custom-call(s32[1]{0:T(128)} %bitcast.place_ref.refs_0_, s32[3,8]{1,0:T(4,128)S(1)} %bitcast.23, f32[256,16,128]{2,1,0:T(8,128)S(1)} %bitcast.17, f32[2,512,128]{2,1,0:T(8,128)S(1)} %collective-permute-done.1.refs_3_, ...), custom_call_target="tpu_custom_call", output_to_operand_aliasing={{}: (12, {})} | custom-call | flops 4294967296 | bytes 4194304 | tf_op jit(solution)/shard_map/pallas_call | solution.py:241
  (2 shorter events, 0.0 us)
Async XLA Ops:
  0.0 6.8 %copy-start.1 = (s32[8,3]{0,1:T(4,128)S(1)}, s32[8,3]{0,1:T(4,128)}, u32[]{:S(2)}) copy-start(s32[8,3]{0,1:T(4,128)} %param.7) | copy-start | bytes 292
  0.0 6.8 %copy-start = (f32[1,256,16,128]{3,2,1,0:T(8,128)S(1)}, f32[1,256,16,128]{3,2,1,0:T(8,128)}, u32[]{:S(2)}) copy-start(f32[1,256,16,128]{3,2,1,0:T(8,128)} %param.4) | copy-start | bytes 6291460
  2.1 13.1 %collective-permute-start.8 = (f32[2,512,128]{2,1,0:T(8,128)}, f32[2,512,128]{2,1,0:T(8,128)}, u32[]{:S(2)}, u32[]{:S(2)}) collective-permute-start(f32[2,512,128]{2,1,0:T(8,128)} %get-tuple-element.19.refs_3_), channel_id=1, source_target_pairs={{16,0},{12,4},{4,8},{24,12},{0,16},{28,20},{20,24},{8,28},{17,1},{... | collective-permute-start | bytes 1572872 | tf_op jit(solution)/shard_map/ppermute | solution.py:35
  5.2 10.1 %collective-permute-start.7 = (f32[2,512,128]{2,1,0:T(8,128)}, f32[2,512,128]{2,1,0:T(8,128)}, u32[]{:S(2)}, u32[]{:S(2)}) collective-permute-start(f32[2,512,128]{2,1,0:T(8,128)} %get-tuple-element.19.refs_3_), channel_id=1, source_target_pairs={{4,0},{0,4},{12,8},{8,12},{20,16},{16,20},{28,24},{24,28},{5,1},{1... | collective-permute-start | bytes 1572872 | tf_op jit(solution)/shard_map/ppermute | solution.py:35
  5.3 14.5 %collective-permute-start = (f32[2,512,128]{2,1,0:T(8,128)}, f32[2,512,128]{2,1,0:T(8,128)S(1)}, u32[]{:S(2)}, u32[]{:S(2)}) collective-permute-start(f32[2,512,128]{2,1,0:T(8,128)} %get-tuple-element.18.refs_4_), channel_id=1, source_target_pairs={{16,0},{12,4},{4,8},{24,12},{0,16},{28,20},{20,24},{8,28},{17,1},{... | collective-permute-start | bytes 1572872 | tf_op jit(solution)/shard_map/ppermute | solution.py:35
  6.8 13.0 %collective-permute-start.2 = (f32[2,512,128]{2,1,0:T(8,128)}, f32[2,512,128]{2,1,0:T(8,128)S(1)}, u32[]{:S(2)}, u32[]{:S(2)}) collective-permute-start(f32[2,512,128]{2,1,0:T(8,128)} %get-tuple-element.18.refs_4_), channel_id=1, source_target_pairs={{4,0},{0,4},{12,8},{8,12},{20,16},{16,20},{28,24},{24,28},{5,1},{1... | collective-permute-start | bytes 1572872 | tf_op jit(solution)/shard_map/ppermute | solution.py:35
  6.8 1.1 %copy-start.2 = (f32[2,512,128]{2,1,0:T(8,128)S(1)}, f32[2,512,128]{2,1,0:T(8,128)}, u32[]{:S(2)}) copy-start(f32[2,512,128]{2,1,0:T(8,128)} %get-tuple-element.18.refs_4_) | copy-start | bytes 1572868
  7.9 1.0 %copy-start.3 = (f32[2,512,128]{2,1,0:T(8,128)S(1)}, f32[2,512,128]{2,1,0:T(8,128)}, u32[]{:S(2)}) copy-start(f32[2,512,128]{2,1,0:T(8,128)} %get-tuple-element.19.refs_3_) | copy-start | bytes 1572868
  14.6 5.1 %collective-permute-start.5 = (f32[2,2,64,128]{3,2,1,0:T(8,128)S(1)}, f32[2,2,64,128]{3,2,1,0:T(8,128)S(1)}, u32[]{:S(2)}, u32[]{:S(2)}) collective-permute-start(f32[2,2,64,128]{3,2,1,0:T(8,128)S(1)} %get-tuple-element.20), channel_id=1, source_target_pairs={{8,0},{20,4},{0,8},{28,12},{24,16},{4,20},{16,24},{12,28},{9,1},{2... | collective-permute-start | bytes 393224 | tf_op jit(solution)/shard_map/ppermute | solution.py:35
  16.5 8.7 %collective-permute-start.9 = (f32[2,512,128]{2,1,0:T(8,128)S(1)}, f32[2,512,128]{2,1,0:T(8,128)S(1)}, u32[]{:S(2)}, u32[]{:S(2)}) collective-permute-start(f32[2,512,128]{2,1,0:T(8,128)S(1)} %shard_map.50), channel_id=1, source_target_pairs={{12,0},{20,4},{24,8},{0,12},{28,16},{4,20},{8,24},{16,28},{13,1},{... | collective-permute-start | bytes 1572872 | tf_op jit(solution)/shard_map/ppermute | solution.py:35
  19.6 1.7 %collective-permute-start.6 = (f32[2,2,64,128]{3,2,1,0:T(8,128)S(1)}, f32[2,2,64,128]{3,2,1,0:T(8,128)S(1)}, u32[]{:S(2)}, u32[]{:S(2)}) collective-permute-start(f32[2,2,64,128]{3,2,1,0:T(8,128)S(1)} %collective-permute-done.5), channel_id=1, source_target_pairs={{4,0},{0,4},{12,8},{8,12},{20,16},{16,20},{28,24},{24,28},{5,1},{1... | collective-permute-start | bytes 393224 | tf_op jit(solution)/shard_map/ppermute | solution.py:35
  19.9 11.0 %collective-permute-start.3 = (f32[2,512,128]{2,1,0:T(8,128)S(1)}, f32[2,512,128]{2,1,0:T(8,128)S(1)}, u32[]{:S(2)}, u32[]{:S(2)}) collective-permute-start(f32[2,512,128]{2,1,0:T(8,128)S(1)} %shard_map.47), channel_id=1, source_target_pairs={{12,0},{20,4},{24,8},{0,12},{28,16},{4,20},{8,24},{16,28},{13,1},{... | collective-permute-start | bytes 1572872 | tf_op jit(solution)/shard_map/ppermute | solution.py:35
  21.3 13.1 %collective-permute-start.11 = (f32[2,512,128]{2,1,0:T(8,128)}, f32[2,512,128]{2,1,0:T(8,128)S(1)}, u32[]{:S(2)}, u32[]{:S(2)}) collective-permute-start(f32[2,512,128]{2,1,0:T(8,128)} %collective-permute-done.8.came_ref.refs_4_.refs_8_), channel_id=1, source_target_pairs={{4,0},{0,4},{12,8},{8,12},{20,16},{16,20},{28,24},{24,28},{5,1},{1... | collective-permute-start | bytes 1572872 | tf_op jit(solution)/shard_map/ppermute | solution.py:35
  21.4 22.9 %collective-permute-start.1 = (f32[2,512,128]{2,1,0:T(8,128)S(1)}, f32[2,512,128]{2,1,0:T(8,128)S(1)}, u32[]{:S(2)}, u32[]{:S(2)}) collective-permute-start(f32[2,512,128]{2,1,0:T(8,128)S(1)} %collective-permute-done.came_ref.refs_4_.refs_9_), channel_id=1, source_target_pairs={{4,0},{0,4},{12,8},{8,12},{20,16},{16,20},{28,24},{24,28},{5,1},{1... | collective-permute-start | bytes 1572872 | tf_op jit(solution)/shard_map/ppermute | solution.py:35
  25.2 14.8 %collective-permute-start.10 = (f32[2,512,128]{2,1,0:T(8,128)S(1)}, f32[2,512,128]{2,1,0:T(8,128)S(1)}, u32[]{:S(2)}, u32[]{:S(2)}) collective-permute-start(f32[2,512,128]{2,1,0:T(8,128)S(1)} %collective-permute-done.9.refs_4_.refs_3_), channel_id=1, source_target_pairs={{4,0},{0,4},{12,8},{8,12},{20,16},{16,20},{28,24},{24,28},{5,1},{1... | collective-permute-start | bytes 1572872 | tf_op jit(solution)/shard_map/ppermute | solution.py:35
  30.8 13.4 %collective-permute-start.4 = (f32[2,512,128]{2,1,0:T(8,128)S(1)}, f32[2,512,128]{2,1,0:T(8,128)S(1)}, u32[]{:S(2)}, u32[]{:S(2)}) collective-permute-start(f32[2,512,128]{2,1,0:T(8,128)S(1)} %collective-permute-done.3.refs_4_), channel_id=1, source_target_pairs={{4,0},{0,4},{12,8},{8,12},{20,16},{16,20},{28,24},{24,28},{5,1},{1... | collective-permute-start | bytes 1572872 | tf_op jit(solution)/shard_map/ppermute | solution.py:35
